TPU v7x, 128 devices: a whole 4x4x4 slice. The times are simulated.
128 devices in a mesh: ctx: 32 (over z, x, y_lo), tp: 4 (over y_hi, core).
Axes of the slice: x: 4, y: 4 (y_hi: 2, y_lo: 2; y = y_hi * 2 + y_lo), z: 4, core: 2. Of those that a mesh axis runs over, the one named last changes fastest.
Arguments:
- signal: bfloat16 [4096, 2048], P('ctx', 'tp'), may hold values from -6 to 6
- gate: bfloat16 [4096, 2048], P('ctx', 'tp'), may hold values from -6 to 6
- filt: bfloat16 [4096, 2048], P('ctx', 'tp'), may hold values from -0.25 to 0.25
- bias: float32 [2048], P('tp'), may hold values from -2 to 2
- doc_ids: int32 [4096], replicated, may hold values from 0 to 3, never falling along the last dimension, each value on 1 to 3840 neighbouring positions
- block_perm: int32 [64], replicated, may hold values from 0 to 63, each once
- out_weight: bfloat16 [2048, 2048], P('tp'), may hold values from -0.125 to 0.125
Outputs:
- mixed: bfloat16 [4096, 2048], P('ctx', 'tp')
Inputs may be any that keep to these rules, and one draw needn't show every extreme that they name: `doc_ids`: ids never fall along the sequence; each document is a run of 1 to 3840 positions, one exactly 3840. `block_perm`: each block number once.
All inputs are finite; a program needn't handle non-finite values.
Results may differ from a plain program's by a relative error of at most 0.012.
Values may be sent and summed in bfloat16 or wider, within the bound.
No kernel may reach another device: no remote copies, remote signals or barrier semaphores. Data moves between devices by JAX's collectives and lax.ppermute only.
A program may use at most 64 MiB of HBM per device.

v0:
```python
import math

import jax
import jax.numpy as jnp
from jax import lax
from jax.sharding import PartitionSpec as P

SPAN = 64


def split_table(table):
    upper_part = table.astype(jnp.bfloat16)
    lower_part = (table - upper_part.astype(jnp.float32)).astype(jnp.bfloat16)
    return (upper_part, lower_part)


def transform_many(divide_pair_table, input_values):
    first_position = jnp.einsum(
        "ol,wld->wod", divide_pair_table[0], input_values, preferred_element_type=jnp.float32
    )
    return first_position + jnp.einsum(
        "ol,wld->wod", divide_pair_table[1], input_values, preferred_element_type=jnp.float32
    )


def group_size():
    return 4


def body(signal, gate, filt, bias, doc_ids, block_perm, out_weight):
    block_len = SPAN
    frame_len = 2 * block_len
    channels = signal.shape[1]
    highest_index = lax.Precision.HIGHEST
    whole_filter = lax.all_gather(filt, "ctx", axis=0, tiled=True)
    positions = jnp.arange(frame_len, dtype=jnp.int32)
    phase_idx = positions[:, None] * positions[None, :] % frame_len
    angles = phase_idx.astype(jnp.float32) * (2.0 * math.pi / frame_len)
    cos_tab = jnp.cos(angles)
    sin_tab = jnp.sin(angles)
    cos_kernel = split_table(cos_tab[:, : frame_len - 1])
    sin_kernel = split_table(sin_tab[:, : frame_len - 1])
    cos_source = split_table(cos_tab[:, :block_len])
    sine_source_rows = split_table(sin_tab[:, :block_len])
    cycle_pos = lax.axis_index("ctx")
    own_blocks = lax.dynamic_slice_in_dim(block_perm, 2 * cycle_pos, 2)
    target_blocks = [own_blocks[0], own_blocks[1]]
    target_docs = [
        lax.dynamic_slice_in_dim(doc_ids, number * block_len, block_len) for number in target_blocks
    ]
    lead_docs = [docs[0] for docs in target_docs]
    own_rows = [signal[:block_len], signal[block_len:]]

    def block_docs(number):
        return lax.dynamic_slice_in_dim(doc_ids, number * block_len, block_len)

    def filter_window(lag_blocks):
        return lax.dynamic_slice_in_dim(
            whole_filter, lag_blocks * block_len - block_len + 1, frame_len - 1, 0
        )

    def pair_spectra(sources, source_numbers, target_numbers, leads):
        source_docs = jax.vmap(block_docs)(source_numbers)
        keep_rows = (source_docs == leads[:, None]) & (source_numbers < target_numbers)[:, None]
        masked = jnp.where(keep_rows[:, :, None], sources, jnp.zeros_like(sources))
        lag_blocks = jnp.maximum(target_numbers - source_numbers, 1)
        windows = jax.vmap(filter_window)(lag_blocks)
        kernel_re = transform_many(cos_kernel, windows)
        kernel_im = -transform_many(sin_kernel, windows)
        source_re = transform_many(cos_source, masked)
        source_im = -transform_many(sine_source_rows, masked)
        return (
            kernel_re * source_re - kernel_im * source_im,
            kernel_re * source_im + kernel_im * source_re,
        )

    def inverse(spec_re, spec_im, docs, lead_doc):
        values = jnp.dot(cos_tab[block_len - 1 : frame_len - 1], spec_re, precision=highest_index)
        values = values - jnp.dot(
            sin_tab[block_len - 1 : frame_len - 1], spec_im, precision=highest_index
        )
        return jnp.where((docs == lead_doc)[:, None], values / frame_len, 0.0)

    zero_spec = jnp.zeros((frame_len, channels), jnp.float32)
    totals = (zero_spec, zero_spec, zero_spec, zero_spec)
    arrived = lax.all_gather(signal, "ctx", axis=0, tiled=True)
    block_count = arrived.shape[0] // block_len
    group = group_size()
    steps = block_count // group
    arrived_groups = arrived.reshape(steps, group, block_len, channels)

    def absorb_group(running, item):
        group_rows, step_index = item
        numbers = lax.dynamic_slice_in_dim(block_perm, step_index * group, group)
        sources = jnp.concatenate([group_rows, group_rows], axis=0)
        source_numbers = jnp.concatenate([numbers, numbers], axis=0)
        target_numbers = jnp.concatenate(
            [
                jnp.full((group,), target_blocks[0], jnp.int32),
                jnp.full((group,), target_blocks[1], jnp.int32),
            ],
            axis=0,
        )
        leads = jnp.concatenate(
            [
                jnp.full((group,), lead_docs[0], jnp.int32),
                jnp.full((group,), lead_docs[1], jnp.int32),
            ],
            axis=0,
        )
        part_re, part_im = pair_spectra(sources, source_numbers, target_numbers, leads)
        part_re = part_re.reshape(2, group, frame_len, channels).sum(axis=1)
        part_im = part_im.reshape(2, group, frame_len, channels).sum(axis=1)
        return (
            (
                running[0] + part_re[0],
                running[1] + part_im[0],
                running[2] + part_re[1],
                running[3] + part_im[1],
            ),
            None,
        )

    totals, unused = lax.scan(
        absorb_group, totals, (arrived_groups, jnp.arange(steps, dtype=jnp.int32))
    )
    distant = [
        inverse(totals[2 * slot], totals[2 * slot + 1], target_docs[slot], lead_docs[slot])
        for slot in range(2)
    ]
    offsets = positions[:block_len][:, None] - positions[:block_len][None, :]
    near_taps = whole_filter[:block_len]
    gathered_taps = near_taps[jnp.maximum(offsets, 0)]
    gated_parts = []
    for slot in range(2):
        docs = target_docs[slot]
        allowed = (offsets >= 0) & (docs[:, None] == docs[None, :])
        toeplitz = jnp.where(allowed[:, :, None], gathered_taps, jnp.zeros_like(gathered_taps))
        local_part = jnp.einsum(
            "tsc,sc->tc", toeplitz, own_rows[slot], preferred_element_type=jnp.float32
        )
        source = own_rows[slot].astype(jnp.float32)
        gate_rows = gate[slot * block_len : (slot + 1) * block_len].astype(jnp.float32)
        gated_parts.append(
            (gate_rows * (local_part + distant[slot] + bias[None, :] * source)).astype(jnp.bfloat16)
        )
    gated = jnp.concatenate(gated_parts, axis=0)
    partial_value = jnp.dot(gated, out_weight, preferred_element_type=jnp.float32)
    return lax.psum_scatter(partial_value, "tp", scatter_dimension=1, tiled=True).astype(
        jnp.bfloat16
    )


def solution(mesh):
    return jax.shard_map(
        body,
        mesh=mesh,
        in_specs=(P("ctx", "tp"), P("ctx", "tp"), P("ctx", "tp"), P("tp"), P(), P(), P("tp", None)),
        out_specs=P("ctx", "tp"),
        check_vma=False,
    )
```

profile of v0, /device:TPU:1, one launch (start us, length us, event | category | flops | bytes accessed | tf_op | source)
XLA Modules:
  0.0 1315.9 jit_solution(3132769725770774739)
XLA Ops:
  22.6 126.9 %all-gather.3.cloned.1.call-done = bf16[4096,512]{1,0:T(8,128)(2,1)} async-done(((bf16[128,512]{1,0:T(8,128)(2,1)}), bf16[4096,512]{1,0:T(8,128)(2,1)}) %all-gather.3.cloned.1.call-update) | async-done | bytes 4194320 | tf_op jit(solution)/shard_map/all_gather | solution.py:35
  149.6 158.3 %all-gather.5.cloned.1.call-done = bf16[4096,512]{1,0:T(8,128)(2,1)} async-done(((bf16[128,512]{1,0:T(8,128)(2,1)}), bf16[4096,512]{1,0:T(8,128)(2,1)}) %all-gather.5.cloned.1.call-update) | async-done | bytes 4194320 | tf_op jit(solution)/shard_map/all_gather | solution.py:86
  308.4 916.3 %while.29 = (s32[]{:T(128)}, f32[128,512]{0,1:T(8,128)}, f32[128,512]{0,1:T(8,128)}, f32[128,512]{0,1:T(8,128)}, f32[128,512]{0,1:T(8,128)}, /*index=5*/s32[]{:T...) while((s32[]{:T(128)}, f32[128,512]{0,1:T(8,128)}, ...), condition=%wide.region_3.4_spmd.clone, body=%wide.region_0.3_spmd.clone.sunk | while | flops 810812544 | bytes 56596156 | solution.py:124
  312.5 17.9 %while.30 = (s32[]{:T(128)}, bf16[4096,512]{1,0:T(8,128)(2,1)}, s32[8,2]{0,1:T(2,128)S(1)}, bf16[8,127,512]{2,1,0:T(8,128)(2,1)S(1)}, s32[]{:T(128)}) while((s32[]{:T(128)}, bf16[4096,512]{1,0:T(8,128)(2,1)}, s32[8,2]{0,1:T(2,128)S(1)}, bf16[8,127,512]{2,1,0:T(8,128)(2,1)S(1)}, s32[]{:T(128)}) %tuple.94), condition=%wide.while_cond, body=%wide.while_body.sunk | while | flops 2 | bytes 261225 | solution.py:58
  339.2 17.1 %while.31 = (s32[]{:T(128)}, s32[4096]{0:T(1024)}, s32[8,1]{0,1:T(1,128)S(1)}, s32[8,64]{1,0:T(8,128)S(1)}, s32[]{:T(128)}, /*index=5*/s32[]{:T(128)}) while((s32[]{:T(128)}, s32[4096]{0:T(1024)}, s32[8,1]{0,1:T(1,128)S(1)}, s32[8,64]{1,0:T(8,128)S(1)}, s32[]{:T(128)}, /*index=5*/s32[]{:T(128)}) %tuple.97), condition=%wide.while_cond.1, body=%wide.while_body.1.sunk | while | flops 2 | bytes 1121 | solution.py:55
  368.7 17.9 %while.30 = (s32[]{:T(128)}, bf16[4096,512]{1,0:T(8,128)(2,1)}, s32[8,2]{0,1:T(2,128)S(1)}, bf16[8,127,512]{2,1,0:T(8,128)(2,1)S(1)}, s32[]{:T(128)}) while((s32[]{:T(128)}, bf16[4096,512]{1,0:T(8,128)(2,1)}, s32[8,2]{0,1:T(2,128)S(1)}, bf16[8,127,512]{2,1,0:T(8,128)(2,1)S(1)}, s32[]{:T(128)}) %tuple.94), condition=%wide.while_cond, body=%wide.while_body.sunk | while | flops 2 | bytes 261225 | solution.py:58
  426.0 17.9 %while.30 = (s32[]{:T(128)}, bf16[4096,512]{1,0:T(8,128)(2,1)}, s32[8,2]{0,1:T(2,128)S(1)}, bf16[8,127,512]{2,1,0:T(8,128)(2,1)S(1)}, s32[]{:T(128)}) while((s32[]{:T(128)}, bf16[4096,512]{1,0:T(8,128)(2,1)}, s32[8,2]{0,1:T(2,128)S(1)}, bf16[8,127,512]{2,1,0:T(8,128)(2,1)S(1)}, s32[]{:T(128)}) %tuple.94), condition=%wide.while_cond, body=%wide.while_body.sunk | while | flops 2 | bytes 261225 | solution.py:58
  452.7 17.1 %while.31 = (s32[]{:T(128)}, s32[4096]{0:T(1024)}, s32[8,1]{0,1:T(1,128)S(1)}, s32[8,64]{1,0:T(8,128)S(1)}, s32[]{:T(128)}, /*index=5*/s32[]{:T(128)}) while((s32[]{:T(128)}, s32[4096]{0:T(1024)}, s32[8,1]{0,1:T(1,128)S(1)}, s32[8,64]{1,0:T(8,128)S(1)}, s32[]{:T(128)}, /*index=5*/s32[]{:T(128)}) %tuple.97), condition=%wide.while_cond.1, body=%wide.while_body.1.sunk | while | flops 2 | bytes 1121 | solution.py:55
  483.4 17.9 %while.30 = (s32[]{:T(128)}, bf16[4096,512]{1,0:T(8,128)(2,1)}, s32[8,2]{0,1:T(2,128)S(1)}, bf16[8,127,512]{2,1,0:T(8,128)(2,1)S(1)}, s32[]{:T(128)}) while((s32[]{:T(128)}, bf16[4096,512]{1,0:T(8,128)(2,1)}, s32[8,2]{0,1:T(2,128)S(1)}, bf16[8,127,512]{2,1,0:T(8,128)(2,1)S(1)}, s32[]{:T(128)}) %tuple.94), condition=%wide.while_cond, body=%wide.while_body.sunk | while | flops 2 | bytes 261225 | solution.py:58
  540.7 17.9 %while.30 = (s32[]{:T(128)}, bf16[4096,512]{1,0:T(8,128)(2,1)}, s32[8,2]{0,1:T(2,128)S(1)}, bf16[8,127,512]{2,1,0:T(8,128)(2,1)S(1)}, s32[]{:T(128)}) while((s32[]{:T(128)}, bf16[4096,512]{1,0:T(8,128)(2,1)}, s32[8,2]{0,1:T(2,128)S(1)}, bf16[8,127,512]{2,1,0:T(8,128)(2,1)S(1)}, s32[]{:T(128)}) %tuple.94), condition=%wide.while_cond, body=%wide.while_body.sunk | while | flops 2 | bytes 261225 | solution.py:58
  598.1 17.9 %while.30 = (s32[]{:T(128)}, bf16[4096,512]{1,0:T(8,128)(2,1)}, s32[8,2]{0,1:T(2,128)S(1)}, bf16[8,127,512]{2,1,0:T(8,128)(2,1)S(1)}, s32[]{:T(128)}) while((s32[]{:T(128)}, bf16[4096,512]{1,0:T(8,128)(2,1)}, s32[8,2]{0,1:T(2,128)S(1)}, bf16[8,127,512]{2,1,0:T(8,128)(2,1)S(1)}, s32[]{:T(128)}) %tuple.94), condition=%wide.while_cond, body=%wide.while_body.sunk | while | flops 2 | bytes 261225 | solution.py:58
  655.4 17.9 %while.30 = (s32[]{:T(128)}, bf16[4096,512]{1,0:T(8,128)(2,1)}, s32[8,2]{0,1:T(2,128)S(1)}, bf16[8,127,512]{2,1,0:T(8,128)(2,1)S(1)}, s32[]{:T(128)}) while((s32[]{:T(128)}, bf16[4096,512]{1,0:T(8,128)(2,1)}, s32[8,2]{0,1:T(2,128)S(1)}, bf16[8,127,512]{2,1,0:T(8,128)(2,1)S(1)}, s32[]{:T(128)}) %tuple.94), condition=%wide.while_cond, body=%wide.while_body.sunk | while | flops 2 | bytes 261225 | solution.py:58
  712.8 17.9 %while.30 = (s32[]{:T(128)}, bf16[4096,512]{1,0:T(8,128)(2,1)}, s32[8,2]{0,1:T(2,128)S(1)}, bf16[8,127,512]{2,1,0:T(8,128)(2,1)S(1)}, s32[]{:T(128)}) while((s32[]{:T(128)}, bf16[4096,512]{1,0:T(8,128)(2,1)}, s32[8,2]{0,1:T(2,128)S(1)}, bf16[8,127,512]{2,1,0:T(8,128)(2,1)S(1)}, s32[]{:T(128)}) %tuple.94), condition=%wide.while_cond, body=%wide.while_body.sunk | while | flops 2 | bytes 261225 | solution.py:58
  739.5 17.1 %while.31 = (s32[]{:T(128)}, s32[4096]{0:T(1024)}, s32[8,1]{0,1:T(1,128)S(1)}, s32[8,64]{1,0:T(8,128)S(1)}, s32[]{:T(128)}, /*index=5*/s32[]{:T(128)}) while((s32[]{:T(128)}, s32[4096]{0:T(1024)}, s32[8,1]{0,1:T(1,128)S(1)}, s32[8,64]{1,0:T(8,128)S(1)}, s32[]{:T(128)}, /*index=5*/s32[]{:T(128)}) %tuple.97), condition=%wide.while_cond.1, body=%wide.while_body.1.sunk | while | flops 2 | bytes 1121 | solution.py:55
  770.1 17.9 %while.30 = (s32[]{:T(128)}, bf16[4096,512]{1,0:T(8,128)(2,1)}, s32[8,2]{0,1:T(2,128)S(1)}, bf16[8,127,512]{2,1,0:T(8,128)(2,1)S(1)}, s32[]{:T(128)}) while((s32[]{:T(128)}, bf16[4096,512]{1,0:T(8,128)(2,1)}, s32[8,2]{0,1:T(2,128)S(1)}, bf16[8,127,512]{2,1,0:T(8,128)(2,1)S(1)}, s32[]{:T(128)}) %tuple.94), condition=%wide.while_cond, body=%wide.while_body.sunk | while | flops 2 | bytes 261225 | solution.py:58
  827.5 17.9 %while.30 = (s32[]{:T(128)}, bf16[4096,512]{1,0:T(8,128)(2,1)}, s32[8,2]{0,1:T(2,128)S(1)}, bf16[8,127,512]{2,1,0:T(8,128)(2,1)S(1)}, s32[]{:T(128)}) while((s32[]{:T(128)}, bf16[4096,512]{1,0:T(8,128)(2,1)}, s32[8,2]{0,1:T(2,128)S(1)}, bf16[8,127,512]{2,1,0:T(8,128)(2,1)S(1)}, s32[]{:T(128)}) %tuple.94), condition=%wide.while_cond, body=%wide.while_body.sunk | while | flops 2 | bytes 261225 | solution.py:58
  884.8 17.9 %while.30 = (s32[]{:T(128)}, bf16[4096,512]{1,0:T(8,128)(2,1)}, s32[8,2]{0,1:T(2,128)S(1)}, bf16[8,127,512]{2,1,0:T(8,128)(2,1)S(1)}, s32[]{:T(128)}) while((s32[]{:T(128)}, bf16[4096,512]{1,0:T(8,128)(2,1)}, s32[8,2]{0,1:T(2,128)S(1)}, bf16[8,127,512]{2,1,0:T(8,128)(2,1)S(1)}, s32[]{:T(128)}) %tuple.94), condition=%wide.while_cond, body=%wide.while_body.sunk | while | flops 2 | bytes 261225 | solution.py:58
  942.1 17.9 %while.30 = (s32[]{:T(128)}, bf16[4096,512]{1,0:T(8,128)(2,1)}, s32[8,2]{0,1:T(2,128)S(1)}, bf16[8,127,512]{2,1,0:T(8,128)(2,1)S(1)}, s32[]{:T(128)}) while((s32[]{:T(128)}, bf16[4096,512]{1,0:T(8,128)(2,1)}, s32[8,2]{0,1:T(2,128)S(1)}, bf16[8,127,512]{2,1,0:T(8,128)(2,1)S(1)}, s32[]{:T(128)}) %tuple.94), condition=%wide.while_cond, body=%wide.while_body.sunk | while | flops 2 | bytes 261225 | solution.py:58
  999.5 17.9 %while.30 = (s32[]{:T(128)}, bf16[4096,512]{1,0:T(8,128)(2,1)}, s32[8,2]{0,1:T(2,128)S(1)}, bf16[8,127,512]{2,1,0:T(8,128)(2,1)S(1)}, s32[]{:T(128)}) while((s32[]{:T(128)}, bf16[4096,512]{1,0:T(8,128)(2,1)}, s32[8,2]{0,1:T(2,128)S(1)}, bf16[8,127,512]{2,1,0:T(8,128)(2,1)S(1)}, s32[]{:T(128)}) %tuple.94), condition=%wide.while_cond, body=%wide.while_body.sunk | while | flops 2 | bytes 261225 | solution.py:58
  1056.8 17.9 %while.30 = (s32[]{:T(128)}, bf16[4096,512]{1,0:T(8,128)(2,1)}, s32[8,2]{0,1:T(2,128)S(1)}, bf16[8,127,512]{2,1,0:T(8,128)(2,1)S(1)}, s32[]{:T(128)}) while((s32[]{:T(128)}, bf16[4096,512]{1,0:T(8,128)(2,1)}, s32[8,2]{0,1:T(2,128)S(1)}, bf16[8,127,512]{2,1,0:T(8,128)(2,1)S(1)}, s32[]{:T(128)}) %tuple.94), condition=%wide.while_cond, body=%wide.while_body.sunk | while | flops 2 | bytes 261225 | solution.py:58
  1114.1 17.9 %while.30 = (s32[]{:T(128)}, bf16[4096,512]{1,0:T(8,128)(2,1)}, s32[8,2]{0,1:T(2,128)S(1)}, bf16[8,127,512]{2,1,0:T(8,128)(2,1)S(1)}, s32[]{:T(128)}) while((s32[]{:T(128)}, bf16[4096,512]{1,0:T(8,128)(2,1)}, s32[8,2]{0,1:T(2,128)S(1)}, bf16[8,127,512]{2,1,0:T(8,128)(2,1)S(1)}, s32[]{:T(128)}) %tuple.94), condition=%wide.while_cond, body=%wide.while_body.sunk | while | flops 2 | bytes 261225 | solution.py:58
  1171.5 17.9 %while.30 = (s32[]{:T(128)}, bf16[4096,512]{1,0:T(8,128)(2,1)}, s32[8,2]{0,1:T(2,128)S(1)}, bf16[8,127,512]{2,1,0:T(8,128)(2,1)S(1)}, s32[]{:T(128)}) while((s32[]{:T(128)}, bf16[4096,512]{1,0:T(8,128)(2,1)}, s32[8,2]{0,1:T(2,128)S(1)}, bf16[8,127,512]{2,1,0:T(8,128)(2,1)S(1)}, s32[]{:T(128)}) %tuple.94), condition=%wide.while_cond, body=%wide.while_body.sunk | while | flops 2 | bytes 261225 | solution.py:58
  1228.5 18.7 %gather_fusion = bf16[4096,512]{1,0:T(8,128)(2,1)} fusion(bf16[64,512]{1,0:T(8,128)(2,1)S(1)} %slice.146, s32[4096]{0:T(1024)} %broadcast_clamp_fusion), kind=kCustom, calls=%fused_computation | custom fusion | bytes 8404992 | tf_op jit(solution)/shard_map/gather | solution.py:133
  1255.9 51.8 %reduce-scatter.2.cloned.1.call-done = f32[128,512]{1,0:T(8,128)} async-done(((f32[128,2048]{1,0:T(8,128)}), f32[128,512]{1,0:T(8,128)}) %reduce-scatter.2.cloned.1.call-update) | async-done | bytes 262160 | tf_op jit(solution)/shard_map/reduce_scatter | solution.py:149
  (1339 shorter events, 1152.2 us)
Async XLA Ops:
  6.5 1247.9 %copy-start = (bf16[512,2048]{1,0:T(8,128)(2,1)S(1)}, bf16[512,2048]{1,0:T(8,128)(2,1)}, u32[]{:S(2)}) copy-start(bf16[512,2048]{1,0:T(8,128)(2,1)} %param.15) | copy-start | bytes 6291460
  6.5 143.0 %all-gather.3.cloned.1.call-start = ((), (), s32[]{:S(2)}) async-start(), calls=%async_computation.1 | async-start | bytes 4325376 | tf_op jit(solution)/shard_map/all_gather | solution.py:35
  7.3 300.6 %all-gather.5.cloned.1.call-start = ((), (), s32[]{:S(2)}) async-start(), calls=%async_computation.2 | async-start | bytes 4325376 | tf_op jit(solution)/shard_map/all_gather | solution.py:86
  8.0 1299.8 %reduce-scatter.2.cloned.1.call-start = ((), (), s32[]{:S(2)}) async-start(), calls=%async_computation.3 | async-start | bytes 1310720 | tf_op jit(solution)/shard_map/reduce_scatter | solution.py:149
  335.5 3.6 copy-start.15
  391.7 3.6 copy-start.15
  449.0 3.6 copy-start.15
  678.4 3.6 copy-start.15
  735.7 3.6 copy-start.15
  965.1 3.6 copy-start.15
  1022.4 3.6 copy-start.15
  1079.8 3.6 copy-start.15
  1137.1 3.6 copy-start.15
  1228.5 18.8 %copy-start.7 = (f32[512,64]{0,1:T(8,128)S(1)}, f32[512,64]{0,1:T(8,128)}, u32[]{:S(2)}) copy-start(f32[512,64]{0,1:T(8,128)} %get-tuple-element.671) | copy-start | bytes 393220
  1228.5 18.8 %copy-start.8 = (f32[512,64]{0,1:T(8,128)S(1)}, f32[512,64]{0,1:T(8,128)}, u32[]{:S(2)}) copy-start(f32[512,64]{0,1:T(8,128)} %get-tuple-element.672) | copy-start | bytes 393220
  1228.5 18.8 %copy-start.10 = (pred[64,64]{1,0:T(8,128)(4,1)S(1)}, pred[64,64]{1,0:T(8,128)(4,1)}, u32[]{:S(2)}) copy-start(pred[64,64]{1,0:T(8,128)(4,1)} %get-tuple-element.675) | copy-start | bytes 12292
  1228.5 18.7 %copy-start.11 = (pred[64,64]{1,0:T(8,128)(4,1)S(1)}, pred[64,64]{1,0:T(8,128)(4,1)}, u32[]{:S(2)}) copy-start(pred[64,64]{1,0:T(8,128)(4,1)} %get-tuple-element.676) | copy-start | bytes 12292
  1247.3 6.1 copy-start.4
  1247.3 6.1 copy-start.5
  1247.3 6.1 copy-start.9
  1247.3 6.1 copy-start.12
  1247.3 6.1 copy-start.14
  1247.3 6.6 copy-start.3
  1247.3 6.6 copy-start.13
  (55 other events, 116.5 us)
Sparse Core Ops, SparseCore 0:
  9.0 140.5 all-gather.2
  151.2 156.5 all-gather.4
  1256.1 51.6 reduce-scatter.1
where the time goes:
time: 1330 us; the launch traced here: 1320 us
  local copies, waits for them, and re-layouts  666 us (50%)
  waiting for transfers between devices  338 us (25%)
  matrix products  204 us (15%)
  other arithmetic  77.2 us (6%)
  loops' own time  15.1 us (1%)
  between operations  14.7 us (1%)
    gather x768, local copies, waits for them, and re-layouts  556 us
    all_gather x1, waiting for transfers between devices, body(): arrived = lax.all_gather(signal, 'ctx', axis=0, tiled=True)  158 us
    all_gather x1, waiting for transfers between devices, body(): whole_filter = lax.all_gather(filt, 'ctx', axis=0, tiled=True)  127 us
    dot_general x64, matrix products, transform_many(): jnp.einsum('ol,wld->wod', divide_pair_table[1], input_values, preferred_e...  114 us
    dot_general x64, matrix products, transform_many(): jnp.einsum('ol,wld->wod', divide_pair_table[0], input_values, preferred_e...  84.9 us
    reduce_scatter x1, waiting for transfers between devices, body(): lax.psum_scatter(partial_value, 'tp', scatter_dimension=1, tiled=True)  51.8 us
    add x16, other arithmetic, absorb_group(): running[3] + part_im[1]  35.1 us
  transfers between devices with their start and end apart: 3, of which 3 were waited for; matrix products, arithmetic and copies ran while one was open for 1% of the time, Pallas kernels for 0%

commit v1 on v0

v1 whole, which is shorter than its diff:
```python
import jax
import jax.numpy as jnp
from jax import lax
from jax.sharding import PartitionSpec as P

SPAN = 64
DOC_COUNT = 4


def skew_blocks(a, fill):
    chans, blocks, span = a.shape
    a_ext = jnp.concatenate([a, jnp.full_like(a, fill)], axis=1)
    tiled = jnp.broadcast_to(a_ext[:, None], (chans, blocks, 2 * blocks, span))
    tiled = tiled.reshape(chans, blocks * 2 * blocks, span)[:, : blocks * (2 * blocks - 1)]
    return tiled.reshape(chans, blocks, 2 * blocks - 1, span)[:, :, :blocks]


def block_conv(x_cm, f_cm, doc_ids):
    chans, seq = x_cm.shape
    span = SPAN
    blocks = seq // span
    width = seq + span
    f_ext = jnp.pad(f_cm, ((0, 0), (0, span)))
    tt = jnp.broadcast_to(f_ext[:, None, :], (chans, span, width)).reshape(chans, span * width)
    tt = tt[:, : span * (width - 1)].reshape(chans, span, width - 1)[:, :, :seq]
    tt = tt.reshape(chans, span, blocks, span)
    xb = x_cm.reshape(chans, blocks, span)
    src = skew_blocks(xb, 0)
    docb = doc_ids.reshape(blocks, span)
    lead = docb[:, 0]
    src_doc = skew_blocks(docb[None], -1)[0]
    keep = src_doc == lead[None, :, None]
    src = jnp.where(keep[None], src, jnp.zeros_like(src))
    lead_part = jnp.einsum("cjdi,cdtj->cit", tt, src, preferred_element_type=jnp.float32)
    row_doc = docb.T
    lead_rows = row_doc == lead[None, :]
    out = jnp.where(lead_rows[None], lead_part, 0.0)
    near = tt[:, :, 0, :]
    xt = jnp.swapaxes(xb, 1, 2)
    for doc in range(DOC_COUNT):
        member = (docb.T == doc)
        part = jnp.einsum(
            "cji,cjt->cit",
            near,
            jnp.where(member[None], xt, jnp.zeros_like(xt)),
            preferred_element_type=jnp.float32,
        )
        rows = member & (lead[None, :] != doc)
        out = out + jnp.where(rows[None], part, 0.0)
    return jnp.swapaxes(out, 1, 2).reshape(chans, seq)


def body(signal, gate, filt, bias, doc_ids, block_perm, out_weight):
    span = SPAN
    rows, chans = signal.shape
    blocks = block_perm.shape[0]
    seq = blocks * span
    n_ctx = seq // rows
    per_dev = chans // n_ctx
    ctx_index = lax.axis_index("ctx")

    def to_channel_major(a):
        return lax.all_to_all(a, "ctx", 1, 0, tiled=True).T

    inverse = jnp.zeros((blocks,), jnp.int32).at[block_perm].set(jnp.arange(blocks, dtype=jnp.int32))

    def slots_to_natural(a):
        return jnp.take(a.reshape(per_dev, blocks, span), inverse, axis=1).reshape(per_dev, seq)

    x_cm = slots_to_natural(to_channel_major(signal))
    g_cm = slots_to_natural(to_channel_major(gate))
    f_cm = to_channel_major(filt)
    bias_cm = lax.dynamic_slice_in_dim(bias, ctx_index * per_dev, per_dev)
    group = 4
    conv = lax.map(
        lambda xf: block_conv(xf[0], xf[1], doc_ids),
        (x_cm.reshape(per_dev // group, group, seq), f_cm.reshape(per_dev // group, group, seq)),
    ).reshape(per_dev, seq)
    gated = (
        g_cm.astype(jnp.float32) * (conv + bias_cm[:, None] * x_cm.astype(jnp.float32))
    ).astype(jnp.bfloat16)
    gated_slots = jnp.take(gated.reshape(per_dev, blocks, span), block_perm, axis=1)
    gated_slots = gated_slots.reshape(per_dev, seq).T
    gated_local = lax.all_to_all(gated_slots, "ctx", 0, 1, tiled=True)
    partial_value = jnp.dot(gated_local, out_weight, preferred_element_type=jnp.float32)
    return lax.psum_scatter(partial_value, "tp", scatter_dimension=1, tiled=True).astype(
        jnp.bfloat16
    )


def solution(mesh):
    return jax.shard_map(
        body,
        mesh=mesh,
        in_specs=(P("ctx", "tp"), P("ctx", "tp"), P("ctx", "tp"), P("tp"), P(), P(), P("tp", None)),
        out_specs=P("ctx", "tp"),
        check_vma=False,
    )
```

time: 1330 us -> 433 us (0.33)
  local copies, waits for them, and re-layouts: 666 us -> 305 us
  waiting for transfers between devices: 338 us -> 39.9 us
  matrix products: 204 us -> 23.5 us
  other arithmetic: 77.2 us -> 12.4 us
  starting transfers between devices: 0.08 us -> 20.6 us
  blocking collectives: 0 us -> 15.1 us
  loops' own time: 15.1 us -> 0.57 us
    gather x769 -> x3, local copies, waits for them, and re-layouts: 575 us -> 1.9 us  [the longest x2 1.27 us: slots_to_natural(): jnp.take(a.reshape(per_dev, blocks, span), inverse, axis=1)]
    all_gather x2 -> x0, waiting for transfers between devices: 285 us -> none  [the longest x1 158 us: body(): arrived = lax.all_gather(signal, 'ctx', axis=0, tiled=True)]
    reshape x0 -> x43, local copies, waits for them, and re-layouts: none -> 204 us  [the longest x8 103 us: skew_blocks(): return tiled.reshape(chans, blocks, 2 * blocks - 1, span)[:, :, :blocks]]
    dot_general x133 -> x21, matrix products: 204 us -> 23.5 us  [the longest x4 19.6 us: block_conv(): jnp.einsum('cjdi,cdtj->cit', tt, src, preferred_element_type=jnp.float32)]
    add x16 -> x0, other arithmetic: 35.1 us -> none  [absorb_group(): running[3] + part_im[1]]
    dynamic_slice x34 -> x5, local copies, waits for them, and re-layouts: 35.1 us -> 1.42 us  [the longest x1 1.33 us: body(): bias_cm = lax.dynamic_slice_in_dim(bias, ctx_index * per_dev, per_dev)]
    while x128 -> x16, local copies, waits for them, and re-layouts: 3.9 us -> 37.3 us
    all_to_all x0 -> x3, starting transfers between devices: none -> 20.5 us  [to_channel_major(): return lax.all_to_all(a, 'ctx', 1, 0, tiled=True).T]
  transfers between devices with their start and end apart: 3 -> 4, of which waited for: 3 -> 3; matrix products, arithmetic and copies ran while one was open for 1% -> 77% of each run, Pallas kernels for 0% -> 0%
where the time goes in v1:
time: 433 us; the launch traced here: 430 us
  local copies, waits for them, and re-layouts  305 us (70%)
  waiting for transfers between devices  39.9 us (9%)
  matrix products  23.5 us (5%)
  starting transfers between devices  20.6 us (5%)
  blocking collectives  15.1 us (3%)
  between operations  13.6 us (3%)
  other arithmetic  12.4 us (3%)
    reshape x8, local copies, waits for them, and re-layouts, skew_blocks(): return tiled.reshape(chans, blocks, 2 * blocks - 1, span)[:, :, :blocks]  103 us
    while x16, local copies, waits for them, and re-layouts  37.3 us
    reduce_scatter x1, waiting for transfers between devices, body(): lax.psum_scatter(partial_value, 'tp', scatter_dimension=1, tiled=True)  33 us
    reshape x4, local copies, waits for them, and re-layouts, skew_blocks(): tiled.reshape(chans, blocks * 2 * blocks, span)  29.3 us
    reshape x4, local copies, waits for them, and re-layouts, block_conv(): tt = tt.reshape(chans, span, blocks, span)  27.6 us
    broadcast_in_dim x20, local copies, waits for them, and re-layouts, skew_blocks(): tiled = jnp.broadcast_to(a_ext[:, None], (chans, blocks, 2 * blocks, span))  27.4 us
    reshape x4, local copies, waits for them, and re-layouts, block_conv(): tt = tt[:, :span * (width - 1)].reshape(chans, span, width - 1)[:, :, :seq]  25.7 us
    all_to_all x3, starting transfers between devices, to_channel_major(): return lax.all_to_all(a, 'ctx', 1, 0, tiled=True).T  20.5 us
  transfers between devices with their start and end apart: 4, of which 3 were waited for; matrix products, arithmetic and copies ran while one was open for 77% of the time, Pallas kernels for 0%

profile of v1, /device:TPU:1, one launch (start us, length us, event | category | flops | bytes accessed | tf_op | source)
XLA Modules:
  0.0 430.1 jit_solution(5247840323906330248)
XLA Ops:
  8.3 9.7 %all-to-all-start.1 = ((bf16[128,32,16]{0,2,1:T(8,128)(2,1)}), bf16[128,32,16]{0,2,1:T(8,128)(2,1)S(1)}, u32[]{:S(2)}, u32[]{:S(2)}) async-start(bf16[128,32,16]{0,2,1:T(8,128)(2,1)} %bitcast.15), calls=%async_computation.1 | async-start | bytes 262144 | tf_op jit(solution)/shard_map/all_to_all | solution.py:63
  25.7 6.9 %all-to-all-start.2 = ((bf16[128,32,16]{0,2,1:T(8,128)(2,1)}), bf16[128,32,16]{0,2,1:T(8,128)(2,1)S(1)}, u32[]{:S(2)}, u32[]{:S(2)}) async-start(bf16[128,32,16]{0,2,1:T(8,128)(2,1)} %bitcast.19), calls=%async_computation.2 | async-start | bytes 262144 | tf_op jit(solution)/shard_map/all_to_all | solution.py:63
  44.2 323.2 %while.12 = (s32[]{:T(128)}, f32[4,4,4096]{2,1,0:T(4,128)}, s32[4096]{0:T(1024)S(1)}, bf16[4,4,4096]{2,1,0:T(4,128)(2,1)S(1)}, bf16[4,4,4096]{2,1,0:T(4,128)(2,1)S(1)}, /*index=5*/s32[]{:T(128)}, bf16[]{:T(256)}) while((s32[]{:T(128)}, f32[4,4,4096]{2,1,0:T(4,128)}, s32[4096]{0:T(1024)S(1)}, bf16[4,4,4096]{2,1,0:T(4,128)(2,1)S(1)}, ...), condition=%wide.region_2.4_spmd, body=%wide.region_1.0_spmd.sunk | while | flops 144167168 | bytes 68822360 | solution.py:75
  59.2 6.4 %reshape.234 = bf16[4,64,4159]{2,1,0:T(8,128)(2,1)} reshape(bf16[1064704]{0:T(1024)(128)(2,1)} %reshape.233) | data formatting | bytes 4258816 | tf_op jit(solution)/shard_map/while/body/eval_jaxpr/reshape | solution.py:25
  68.8 6.9 %reshape.235 = bf16[4,64,64,64]{3,2,1,0:T(8,128)(2,1)} reshape(bf16[4,64,4096]{2,1,0:T(8,128)(2,1)} %slice.80) | data formatting | bytes 4194304 | tf_op jit(solution)/shard_map/while/body/eval_jaxpr/reshape | solution.py:26
  80.0 7.3 %reshape.238 = bf16[4,8192,64]{1,2,0:T(8,128)(2,1)} reshape(bf16[4,64,128,64]{2,1,3,0:T(8,128)(2,1)} %broadcast_in_dim.226) | data formatting | bytes 8388608 | tf_op jit(solution)/shard_map/while/body/eval_jaxpr/reshape | solution.py:14
  87.4 19.3 %reshape.239 = bf16[4,64,127,64]{2,1,3,0:T(8,128)(2,1)} reshape(bf16[4,8128,64]{1,2,0:T(8,128)(2,1)} %bitcast.133) | data formatting | bytes 8323072 | tf_op jit(solution)/shard_map/while/body/eval_jaxpr/reshape | solution.py:15
  111.1 6.4 %reshape.241 = s32[1,64,127,64]{2,1,3,0:T(8,128)} reshape(s32[1,8128,64]{1,2,0:T(8,128)} %bitcast.135) | data formatting | bytes 4161536 | tf_op jit(solution)/shard_map/while/body/eval_jaxpr/reshape | solution.py:15
  140.0 6.4 %reshape.234 = bf16[4,64,4159]{2,1,0:T(8,128)(2,1)} reshape(bf16[1064704]{0:T(1024)(128)(2,1)} %reshape.233) | data formatting | bytes 4258816 | tf_op jit(solution)/shard_map/while/body/eval_jaxpr/reshape | solution.py:25
  149.5 6.9 %reshape.235 = bf16[4,64,64,64]{3,2,1,0:T(8,128)(2,1)} reshape(bf16[4,64,4096]{2,1,0:T(8,128)(2,1)} %slice.80) | data formatting | bytes 4194304 | tf_op jit(solution)/shard_map/while/body/eval_jaxpr/reshape | solution.py:26
  160.8 7.3 %reshape.238 = bf16[4,8192,64]{1,2,0:T(8,128)(2,1)} reshape(bf16[4,64,128,64]{2,1,3,0:T(8,128)(2,1)} %broadcast_in_dim.226) | data formatting | bytes 8388608 | tf_op jit(solution)/shard_map/while/body/eval_jaxpr/reshape | solution.py:14
  168.1 19.3 %reshape.239 = bf16[4,64,127,64]{2,1,3,0:T(8,128)(2,1)} reshape(bf16[4,8128,64]{1,2,0:T(8,128)(2,1)} %bitcast.133) | data formatting | bytes 8323072 | tf_op jit(solution)/shard_map/while/body/eval_jaxpr/reshape | solution.py:15
  191.8 6.4 %reshape.241 = s32[1,64,127,64]{2,1,3,0:T(8,128)} reshape(s32[1,8128,64]{1,2,0:T(8,128)} %bitcast.135) | data formatting | bytes 4161536 | tf_op jit(solution)/shard_map/while/body/eval_jaxpr/reshape | solution.py:15
  220.7 6.4 %reshape.234 = bf16[4,64,4159]{2,1,0:T(8,128)(2,1)} reshape(bf16[1064704]{0:T(1024)(128)(2,1)} %reshape.233) | data formatting | bytes 4258816 | tf_op jit(solution)/shard_map/while/body/eval_jaxpr/reshape | solution.py:25
  230.3 6.9 %reshape.235 = bf16[4,64,64,64]{3,2,1,0:T(8,128)(2,1)} reshape(bf16[4,64,4096]{2,1,0:T(8,128)(2,1)} %slice.80) | data formatting | bytes 4194304 | tf_op jit(solution)/shard_map/while/body/eval_jaxpr/reshape | solution.py:26
  241.6 7.3 %reshape.238 = bf16[4,8192,64]{1,2,0:T(8,128)(2,1)} reshape(bf16[4,64,128,64]{2,1,3,0:T(8,128)(2,1)} %broadcast_in_dim.226) | data formatting | bytes 8388608 | tf_op jit(solution)/shard_map/while/body/eval_jaxpr/reshape | solution.py:14
  248.9 19.3 %reshape.239 = bf16[4,64,127,64]{2,1,3,0:T(8,128)(2,1)} reshape(bf16[4,8128,64]{1,2,0:T(8,128)(2,1)} %bitcast.133) | data formatting | bytes 8323072 | tf_op jit(solution)/shard_map/while/body/eval_jaxpr/reshape | solution.py:15
  272.6 6.4 %reshape.241 = s32[1,64,127,64]{2,1,3,0:T(8,128)} reshape(s32[1,8128,64]{1,2,0:T(8,128)} %bitcast.135) | data formatting | bytes 4161536 | tf_op jit(solution)/shard_map/while/body/eval_jaxpr/reshape | solution.py:15
  301.5 6.4 %reshape.234 = bf16[4,64,4159]{2,1,0:T(8,128)(2,1)} reshape(bf16[1064704]{0:T(1024)(128)(2,1)} %reshape.233) | data formatting | bytes 4258816 | tf_op jit(solution)/shard_map/while/body/eval_jaxpr/reshape | solution.py:25
  311.0 6.9 %reshape.235 = bf16[4,64,64,64]{3,2,1,0:T(8,128)(2,1)} reshape(bf16[4,64,4096]{2,1,0:T(8,128)(2,1)} %slice.80) | data formatting | bytes 4194304 | tf_op jit(solution)/shard_map/while/body/eval_jaxpr/reshape | solution.py:26
  322.3 7.3 %reshape.238 = bf16[4,8192,64]{1,2,0:T(8,128)(2,1)} reshape(bf16[4,64,128,64]{2,1,3,0:T(8,128)(2,1)} %broadcast_in_dim.226) | data formatting | bytes 8388608 | tf_op jit(solution)/shard_map/while/body/eval_jaxpr/reshape | solution.py:14
  329.7 19.3 %reshape.239 = bf16[4,64,127,64]{2,1,3,0:T(8,128)(2,1)} reshape(bf16[4,8128,64]{1,2,0:T(8,128)(2,1)} %bitcast.133) | data formatting | bytes 8323072 | tf_op jit(solution)/shard_map/while/body/eval_jaxpr/reshape | solution.py:15
  372.1 15.1 %all_to_all.76 = bf16[32,128,16]{1,2,0:T(8,128)(2,1)S(1)} all-to-all(bf16[32,128,16]{1,2,0:T(8,128)(2,1)S(1)} %copy_bitcast_fusion.1), channel_id=1, replica_groups=mesh['ctx'=32,'tp'=4] {'ctx'}, dimensions={0} | all-to-all | bytes 262144 | tf_op jit(solution)/shard_map/all_to_all | solution.py:84
  388.6 33.0 %reduce-scatter.2.cloned.1.call-done = f32[128,512]{1,0:T(8,128)} async-done(((f32[128,2048]{1,0:T(8,128)}), f32[128,512]{1,0:T(8,128)}) %reduce-scatter.2.cloned.1.call-update) | async-done | bytes 262160 | tf_op jit(solution)/shard_map/reduce_scatter | solution.py:86
  (170 shorter events, 172.3 us)
Async XLA Ops:
  6.5 380.6 %copy-start = (bf16[512,2048]{1,0:T(8,128)(2,1)S(1)}, bf16[512,2048]{1,0:T(8,128)(2,1)}, u32[]{:S(2)}) copy-start(bf16[512,2048]{1,0:T(8,128)(2,1)} %param.17) | copy-start | bytes 6291460
  8.3 17.3 %all-to-all-start.1 = ((bf16[128,32,16]{0,2,1:T(8,128)(2,1)}), bf16[128,32,16]{0,2,1:T(8,128)(2,1)S(1)}, u32[]{:S(2)}, u32[]{:S(2)}) async-start(bf16[128,32,16]{0,2,1:T(8,128)(2,1)} %bitcast.15), calls=%async_computation.1 | async-start | bytes 262144 | tf_op jit(solution)/shard_map/all_to_all | solution.py:63
  23.6 20.7 %copy-start.1 = (s32[4096]{0:T(1024)S(1)}, s32[4096]{0:T(1024)}, u32[]{:S(2)}) copy-start(s32[4096]{0:T(1024)} %param.15) | copy-start | bytes 49156
  25.7 14.5 %all-to-all-start.2 = ((bf16[128,32,16]{0,2,1:T(8,128)(2,1)}), bf16[128,32,16]{0,2,1:T(8,128)(2,1)S(1)}, u32[]{:S(2)}, u32[]{:S(2)}) async-start(bf16[128,32,16]{0,2,1:T(8,128)(2,1)} %bitcast.19), calls=%async_computation.2 | async-start | bytes 262144 | tf_op jit(solution)/shard_map/all_to_all | solution.py:63
  40.2 328.5 %all-to-all-start = ((bf16[128,32,16]{0,2,1:T(8,128)(2,1)}), bf16[128,32,16]{0,2,1:T(8,128)(2,1)S(1)}, u32[]{:S(2)}, u32[]{:S(2)}) async-start(bf16[128,32,16]{0,2,1:T(8,128)(2,1)} %bitcast.11), calls=%async_computation | async-start | bytes 262144 | tf_op jit(solution)/shard_map/all_to_all | solution.py:63
  44.1 377.6 %reduce-scatter.2.cloned.1.call-start = ((), (), s32[]{:S(2)}) async-start(), calls=%async_computation.5 | async-start | bytes 1310720 | tf_op jit(solution)/shard_map/reduce_scatter | solution.py:86
Sparse Core Ops, SparseCore 0:
  388.7 32.8 reduce-scatter.1

commit v2 on v1

v2 whole, which is shorter than its diff:
```python
import jax
import jax.numpy as jnp
from jax import lax
from jax.experimental import pallas as pl
from jax.experimental.pallas import tpu as pltpu
from jax.sharding import PartitionSpec as P

SPAN = 64
DOC_COUNT = 4


def conv_kernel(f_ref, x_ref, doc_ref, mz_ref, y_ref):
    blocks, span = x_ref.shape[1], x_ref.shape[2]
    seq = blocks * span
    width = f_ref.shape[2]
    lanes = 2 * span
    fb = jnp.broadcast_to(f_ref[0].astype(jnp.float32), (span, width))
    tt = pltpu.roll(fb, 0, 1, stride=1, stride_axis=0)[:, :seq].astype(jnp.bfloat16)
    x = x_ref[0]
    docs = doc_ref[...]
    lead = docs[:, 0:1]
    last = docs[:, span - 1 : span]
    zero = jnp.zeros_like(x)
    x_lead = jnp.where(docs == lead, x, zero)
    x_last = jnp.where((docs == last) & (docs != lead), x, zero)
    z_lead = jnp.dot(x_lead, tt, preferred_element_type=jnp.float32)
    z_last = jnp.dot(x_last, tt, preferred_element_type=jnp.float32)
    zm = z_lead * mz_ref[0] + z_last * mz_ref[1]
    acc = zm[:, :lanes]
    for pair in range(1, seq // lanes):
        acc = acc + pltpu.roll(zm[:, pair * lanes : (pair + 1) * lanes], 2 * pair, 0)
    y = acc[:, :span] + pltpu.roll(acc[:, span:], 1, 0)
    near = tt[:, :span]
    planes = jnp.concatenate([jnp.where(docs == doc, x, zero) for doc in range(DOC_COUNT)], axis=0)
    local = jnp.dot(planes, near, preferred_element_type=jnp.float32)
    for doc in range(DOC_COUNT):
        y = y + jnp.where(docs == doc, local[doc * blocks : (doc + 1) * blocks], 0.0)
    y_ref[0] = y


def pallas_conv(x_cm, f_cm, doc_ids):
    chans, seq = x_cm.shape
    span = SPAN
    blocks = seq // span
    width = seq + 2 * span
    f_ext = jnp.pad(f_cm, ((0, 0), (0, width - seq))).reshape(chans, 1, width)
    xb = x_cm.reshape(chans, blocks, span)
    docb = doc_ids.reshape(blocks, span)
    ends = jnp.sum(doc_ids[None, None, :] <= jnp.stack([docb[:, 0], docb[:, -1]])[:, :, None], axis=2)
    rel = lax.broadcasted_iota(jnp.int32, (blocks, seq), 1)
    pos = rel + span * lax.broadcasted_iota(jnp.int32, (blocks, seq), 0)
    mz = ((rel >= span)[None] & (pos[None] < ends[:, :, None])).astype(jnp.float32)
    out = pl.pallas_call(
        conv_kernel,
        grid=(chans,),
        in_specs=[
            pl.BlockSpec((1, 1, width), lambda c: (c, 0, 0)),
            pl.BlockSpec((1, blocks, span), lambda c: (c, 0, 0)),
            pl.BlockSpec((blocks, span), lambda c: (0, 0)),
            pl.BlockSpec((2, blocks, seq), lambda c: (0, 0, 0)),
        ],
        out_specs=pl.BlockSpec((1, blocks, span), lambda c: (c, 0, 0)),
        out_shape=jax.ShapeDtypeStruct((chans, blocks, span), jnp.float32),
    )(f_ext, xb, docb, mz)
    return out.reshape(chans, seq)


def body(signal, gate, filt, bias, doc_ids, block_perm, out_weight):
    span = SPAN
    rows, chans = signal.shape
    blocks = block_perm.shape[0]
    seq = blocks * span
    n_ctx = seq // rows
    per_dev = chans // n_ctx
    ctx_index = lax.axis_index("ctx")

    def to_channel_major(a):
        return lax.all_to_all(a, "ctx", 1, 0, tiled=True).T

    inverse = jnp.zeros((blocks,), jnp.int32).at[block_perm].set(jnp.arange(blocks, dtype=jnp.int32))

    def slots_to_natural(a):
        return jnp.take(a.reshape(per_dev, blocks, span), inverse, axis=1).reshape(per_dev, seq)

    x_cm = slots_to_natural(to_channel_major(signal))
    g_cm = slots_to_natural(to_channel_major(gate))
    f_cm = to_channel_major(filt)
    bias_cm = lax.dynamic_slice_in_dim(bias, ctx_index * per_dev, per_dev)
    conv = pallas_conv(x_cm, f_cm, doc_ids)
    gated = (
        g_cm.astype(jnp.float32) * (conv + bias_cm[:, None] * x_cm.astype(jnp.float32))
    ).astype(jnp.bfloat16)
    gated_slots = jnp.take(gated.reshape(per_dev, blocks, span), block_perm, axis=1)
    gated_slots = gated_slots.reshape(per_dev, seq).T
    gated_local = lax.all_to_all(gated_slots, "ctx", 0, 1, tiled=True)
    partial_value = jnp.dot(gated_local, out_weight, preferred_element_type=jnp.float32)
    return lax.psum_scatter(partial_value, "tp", scatter_dimension=1, tiled=True).astype(
        jnp.bfloat16
    )


def solution(mesh):
    return jax.shard_map(
        body,
        mesh=mesh,
        in_specs=(P("ctx", "tp"), P("ctx", "tp"), P("ctx", "tp"), P("tp"), P(), P(), P("tp", None)),
        out_specs=P("ctx", "tp"),
        check_vma=False,
    )
```

time: 433 us -> 129 us (0.30)
  local copies, waits for them, and re-layouts: 305 us -> 10.1 us
  matrix products: 23.5 us -> 1.46 us
  Pallas kernels: 0 us -> 13.9 us
  waiting for transfers between devices: 39.9 us -> 47.3 us
    reshape x38 -> x3, local copies, waits for them, and re-layouts: 203 us -> 1.72 us  [the longest x2 0.93 us: pallas_conv(): f_ext = jnp.pad(f_cm, ((0, 0), (0, width - seq))).reshape(chans, 1, width)]
    while x16 -> x0, local copies, waits for them, and re-layouts: 37.3 us -> none
    broadcast_in_dim x28 -> x0, local copies, waits for them, and re-layouts: 33.9 us -> none  [the longest x20 27.4 us: skew_blocks(): tiled = jnp.broadcast_to(a_ext[:, None], (chans, blocks, 2 * blocks, span))]
    dot_general x20 -> x0, matrix products: 22 us -> none  [the longest x4 19.6 us: block_conv(): jnp.einsum('cjdi,cdtj->cit', tt, src, preferred_element_type=jnp.float32)]
    slice x12 -> x1, local copies, waits for them, and re-layouts: 17.4 us -> 0.17 us  [pallas_conv(): docb[:, 0]]
    pallas_call x0 -> x1, Pallas kernels: none -> 13.9 us  [pallas_conv(): pl.pallas_call(conv_kernel, grid=(chans,), in_specs=[pl.BlockSpec((1, 1,...]
    broadcast_in_dim x5 -> x0, other arithmetic: 7.53 us -> none  [the longest x4 7.52 us: block_conv(): src = jnp.where(keep[None], src, jnp.zeros_like(src))]
    all_to_all x3, waiting for transfers between devices: 6.85 us -> 13.7 us  [to_channel_major(): return lax.all_to_all(a, 'ctx', 1, 0, tiled=True).T]
  transfers between devices with their start and end apart: 4 -> 4, of which waited for: 3 -> 3; matrix products, arithmetic and copies ran while one was open for 77% -> 8% of each run, Pallas kernels for 0% -> 0%
where the time goes in v2:
time: 129 us; the launch traced here: 127 us
  waiting for transfers between devices  47.3 us (37%)
  starting transfers between devices  21.4 us (17%)
  Pallas kernels  13.9 us (11%)
  between operations  13.6 us (11%)
  blocking collectives  11.1 us (9%)
  local copies, waits for them, and re-layouts  10.1 us (8%)
  other arithmetic  8.16 us (6%)
  matrix products  1.46 us (1%)
    reduce_scatter x1, waiting for transfers between devices, body(): lax.psum_scatter(partial_value, 'tp', scatter_dimension=1, tiled=True)  33.6 us
    all_to_all x3, starting transfers between devices, to_channel_major(): return lax.all_to_all(a, 'ctx', 1, 0, tiled=True).T  21.3 us
    pallas_call x1, Pallas kernels, pallas_conv(): pl.pallas_call(conv_kernel, grid=(chans,), in_specs=[pl.BlockSpec((1, 1,...  13.9 us
    all_to_all x3, waiting for transfers between devices, to_channel_major(): return lax.all_to_all(a, 'ctx', 1, 0, tiled=True).T  13.7 us
    all_to_all x1, blocking collectives, body(): gated_local = lax.all_to_all(gated_slots, 'ctx', 0, 1, tiled=True)  11.1 us
    unnamed x11, local copies, waits for them, and re-layouts  3.36 us
  transfers between devices with their start and end apart: 4, of which 3 were waited for; matrix products, arithmetic and copies ran while one was open for 8% of the time, Pallas kernels for 0%

profile of v2, /device:TPU:1, one launch (start us, length us, event | category | flops | bytes accessed | tf_op | source)
XLA Modules:
  0.0 126.9 jit_solution(2863012753156181067)
XLA Ops:
  6.5 1.8 %copy.52 = bf16[128,512]{0,1:T(8,128)(2,1)} copy(bf16[128,512]{1,0:T(8,128)(2,1)} %param.9) | data formatting | bytes 262144 | tf_op args[0]
  8.4 9.7 %all-to-all-start.2 = ((bf16[128,32,16]{0,2,1:T(8,128)(2,1)}), bf16[128,32,16]{0,2,1:T(8,128)(2,1)S(1)}, u32[]{:S(2)}, u32[]{:S(2)}) async-start(bf16[128,32,16]{0,2,1:T(8,128)(2,1)} %bitcast.8), calls=%async_computation.2 | async-start | bytes 262144 | tf_op jit(solution)/shard_map/all_to_all | solution.py:78
  18.1 0.7 compare_select_fusion
  18.7 0.8 scatter_custom_fusion
  19.6 0.7 compare_and_fusion
  20.2 0.8 reshape.64.doc_ref
  21.2 1.1 convert_reduce_fusion
  22.5 1.7 %and_convert_fusion.mz_ref = f32[2,64,4096]{2,1,0:T(8,128)} fusion(s32[2,64]{1,0:T(2,128)S(1)} %convert_reduce_fusion, s32[64,4096]{1,0:T(8,128)S(1)} %iota_add_fusion, pred[4096]{0:T(1024)(128)(4,1)S(1)} %iota_compare_fusion), kind=kLoop, calls=%fused_computation.5 | loop fusion | flops 1572864 | bytes 3150336 | tf_op jit(solution)/shard_map/convert_element_type | solution.py:52
  24.2 0.8 copy.50
  25.0 0.8 copy.46
  25.8 0.8 dynamic_slice.3
  26.5 7.7 %all-to-all-start.1 = ((bf16[128,32,16]{0,2,1:T(8,128)(2,1)}), bf16[128,32,16]{0,2,1:T(8,128)(2,1)S(1)}, u32[]{:S(2)}, u32[]{:S(2)}) async-start(bf16[128,32,16]{0,2,1:T(8,128)(2,1)} %bitcast.4), calls=%async_computation.1 | async-start | bytes 262144 | tf_op jit(solution)/shard_map/all_to_all | solution.py:78
  34.3 7.5 %all-to-all-done.1 = bf16[128,32,16]{0,2,1:T(8,128)(2,1)S(1)} async-done(((bf16[128,32,16]{0,2,1:T(8,128)(2,1)}), bf16[128,32,16]{0,2,1:T(8,128)(2,1)S(1)}, u32[]{:S(2)}, u32[]{:S(2)}) %all-to-all-start.1) | async-done | bytes 131104 | tf_op jit(solution)/shard_map/all_to_all | solution.py:78
  41.8 3.9 %all-to-all-start = ((bf16[128,32,16]{0,2,1:T(8,128)(2,1)}), bf16[128,32,16]{0,2,1:T(8,128)(2,1)S(1)}, u32[]{:S(2)}, u32[]{:S(2)}) async-start(bf16[128,32,16]{0,2,1:T(8,128)(2,1)} %bitcast), calls=%async_computation | async-start | bytes 262144 | tf_op jit(solution)/shard_map/all_to_all | solution.py:78
  46.2 0.9 copy.56.f_ref
  47.1 6.1 %all-to-all-done = bf16[128,32,16]{0,2,1:T(8,128)(2,1)S(1)} async-done(((bf16[128,32,16]{0,2,1:T(8,128)(2,1)}), bf16[128,32,16]{0,2,1:T(8,128)(2,1)S(1)}, u32[]{:S(2)}, u32[]{:S(2)}) %all-to-all-start) | async-done | bytes 131104 | tf_op jit(solution)/shard_map/all_to_all | solution.py:78
  54.3 0.6 gather_fusion
  55.0 0.8 fusion.x_ref
  55.8 13.9 %shard_map.73 = f32[16,64,64]{2,1,0:T(8,128)} custom-call(bf16[16,1,4224]{2,1,0:T(2,128)(2,1)} %copy.56.f_ref, bf16[16,64,64]{2,1,0:T(8,128)(2,1)} %fusion.x_ref, s32[64,64]{1,0:T(8,128)} %copy-done.1, f32[2,64,4096]{2,1,0:T(8,128)} %and_convert_fusion.mz_ref), custom_call_target="tpu_custom_call" | custom-call | tf_op jit(solution)/shard_map/pallas_call | solution.py:53
  69.7 1.3 multiply_convert_fusion
  72.3 11.1 %all_to_all.76 = bf16[32,128,16]{1,2,0:T(8,128)(2,1)S(1)} all-to-all(bf16[32,128,16]{1,2,0:T(8,128)(2,1)S(1)} %copy_bitcast_fusion), channel_id=1, replica_groups=mesh['ctx'=32,'tp'=4] {'ctx'}, dimensions={0} | all-to-all | bytes 262144 | tf_op jit(solution)/shard_map/all_to_all | solution.py:95
  83.4 1.5 %fusion.3 = f32[128,2048]{1,0:T(8,128)} fusion(bf16[128,512]{0,1:T(8,128)(2,1)S(1)} %bitcast.50, bf16[512,2048]{1,0:T(8,128)(2,1)S(1)} %copy-done), kind=kOutput, calls=%fused_computation.30 | convolution fusion | flops 268435456 | bytes 3276800 | tf_op jit(solution)/shard_map/dot_general | solution.py:96
  84.9 33.6 %reduce-scatter.2.cloned.1.call-done = f32[128,512]{1,0:T(8,128)} async-done(((f32[128,2048]{1,0:T(8,128)}), f32[128,512]{1,0:T(8,128)}) %reduce-scatter.2.cloned.1.call-update) | async-done | bytes 262160 | tf_op jit(solution)/shard_map/reduce_scatter | solution.py:97
  118.4 1.6 %convert_element_type.28 = bf16[128,512]{1,0:T(8,128)(2,1)} convert(f32[128,512]{1,0:T(8,128)} %reduce-scatter.2.cloned.1.call-done) | non-fusion elementwise | flops 65536 | bytes 393216 | tf_op jit(solution)/shard_map/convert_element_type | solution.py:97
  (36 shorter events, 3.2 us)
Async XLA Ops:
  6.5 76.8 %copy-start = (bf16[512,2048]{1,0:T(8,128)(2,1)S(1)}, bf16[512,2048]{1,0:T(8,128)(2,1)}, u32[]{:S(2)}) copy-start(bf16[512,2048]{1,0:T(8,128)(2,1)} %param.15) | copy-start | bytes 6291460
  8.4 18.2 %all-to-all-start.2 = ((bf16[128,32,16]{0,2,1:T(8,128)(2,1)}), bf16[128,32,16]{0,2,1:T(8,128)(2,1)S(1)}, u32[]{:S(2)}, u32[]{:S(2)}) async-start(bf16[128,32,16]{0,2,1:T(8,128)(2,1)} %bitcast.8), calls=%async_computation.2 | async-start | bytes 262144 | tf_op jit(solution)/shard_map/all_to_all | solution.py:78
  21.0 3.2 %copy-start.1 = (s32[64,64]{1,0:T(8,128)}, s32[64,64]{1,0:T(8,128)S(1)}, u32[]{:S(2)}) copy-start(s32[64,64]{1,0:T(8,128)S(1)} %reshape.64.doc_ref) | copy-start | bytes 49156
  22.3 1.9 %copy-start.2 = (bf16[128,512]{1,0:T(8,128)(2,1)S(1)}, bf16[128,512]{1,0:T(8,128)(2,1)}, u32[]{:S(2)}) copy-start(bf16[128,512]{1,0:T(8,128)(2,1)} %param.11) | copy-start | bytes 393220
  22.3 2.7 %copy-start.3 = (bf16[128,512]{1,0:T(8,128)(2,1)S(1)}, bf16[128,512]{1,0:T(8,128)(2,1)}, u32[]{:S(2)}) copy-start(bf16[128,512]{1,0:T(8,128)(2,1)} %param.10) | copy-start | bytes 393220
  26.5 15.3 %all-to-all-start.1 = ((bf16[128,32,16]{0,2,1:T(8,128)(2,1)}), bf16[128,32,16]{0,2,1:T(8,128)(2,1)S(1)}, u32[]{:S(2)}, u32[]{:S(2)}) async-start(bf16[128,32,16]{0,2,1:T(8,128)(2,1)} %bitcast.4), calls=%async_computation.1 | async-start | bytes 262144 | tf_op jit(solution)/shard_map/all_to_all | solution.py:78
  41.8 11.4 %all-to-all-start = ((bf16[128,32,16]{0,2,1:T(8,128)(2,1)}), bf16[128,32,16]{0,2,1:T(8,128)(2,1)S(1)}, u32[]{:S(2)}, u32[]{:S(2)}) async-start(bf16[128,32,16]{0,2,1:T(8,128)(2,1)} %bitcast), calls=%async_computation | async-start | bytes 262144 | tf_op jit(solution)/shard_map/all_to_all | solution.py:78
  45.7 72.8 %reduce-scatter.2.cloned.1.call-start = ((), (), s32[]{:S(2)}) async-start(), calls=%async_computation.5 | async-start | bytes 1310720 | tf_op jit(solution)/shard_map/reduce_scatter | solution.py:97
Sparse Core Ops, SparseCore 0:
  85.0 33.4 reduce-scatter.1

commit v3 on v2

--- a/solution.py
+++ b/solution.py
@@ -74,17 +74,18 @@
     per_dev = chans // n_ctx
     ctx_index = lax.axis_index("ctx")
 
-    def to_channel_major(a):
-        return lax.all_to_all(a, "ctx", 1, 0, tiled=True).T
-
     inverse = jnp.zeros((blocks,), jnp.int32).at[block_perm].set(jnp.arange(blocks, dtype=jnp.int32))
 
     def slots_to_natural(a):
         return jnp.take(a.reshape(per_dev, blocks, span), inverse, axis=1).reshape(per_dev, seq)
 
-    x_cm = slots_to_natural(to_channel_major(signal))
-    g_cm = slots_to_natural(to_channel_major(gate))
-    f_cm = to_channel_major(filt)
+    packed = jnp.stack(
+        [a.reshape(rows, n_ctx, per_dev) for a in (signal, gate, filt)], axis=2
+    ).reshape(rows, n_ctx * 3 * per_dev)
+    arrived = lax.all_to_all(packed, "ctx", 1, 0, tiled=True).T
+    x_cm = slots_to_natural(arrived[:per_dev])
+    g_cm = slots_to_natural(arrived[per_dev : 2 * per_dev])
+    f_cm = arrived[2 * per_dev :]
     bias_cm = lax.dynamic_slice_in_dim(bias, ctx_index * per_dev, per_dev)
     conv = pallas_conv(x_cm, f_cm, doc_ids)
     gated = (
@@ -93,10 +94,19 @@
     gated_slots = jnp.take(gated.reshape(per_dev, blocks, span), block_perm, axis=1)
     gated_slots = gated_slots.reshape(per_dev, seq).T
     gated_local = lax.all_to_all(gated_slots, "ctx", 0, 1, tiled=True)
-    partial_value = jnp.dot(gated_local, out_weight, preferred_element_type=jnp.float32)
-    return lax.psum_scatter(partial_value, "tp", scatter_dimension=1, tiled=True).astype(
-        jnp.bfloat16
-    )
+    tp_index = lax.axis_index("tp")
+    n_tp = out_weight.shape[1] // chans
+    high, core = tp_index // 2, tp_index % 2
+    half = out_weight.shape[1] // 2
+    w_other = lax.dynamic_slice_in_dim(out_weight, (1 - high) * half, half, axis=1)
+    p_other = jnp.dot(gated_local, w_other, preferred_element_type=jnp.float32)
+    recv_high = lax.ppermute(p_other, "tp", [(i, i ^ 2) for i in range(n_tp)])
+    w_mine = lax.dynamic_slice_in_dim(out_weight, high * half, half, axis=1)
+    p_mine = jnp.dot(gated_local, w_mine, preferred_element_type=jnp.float32) + recv_high
+    send_core = lax.dynamic_slice_in_dim(p_mine, (1 - core) * chans, chans, axis=1)
+    keep_core = lax.dynamic_slice_in_dim(p_mine, core * chans, chans, axis=1)
+    recv_core = lax.ppermute(send_core, "tp", [(i, i ^ 1) for i in range(n_tp)])
+    return (keep_core + recv_core).astype(jnp.bfloat16)
 
 
 def solution(mesh):

time: 129 us -> 76.3 us (0.59)
  waiting for transfers between devices: 47.3 us -> 23.9 us
  between operations: 13.6 us -> 0.27 us
  blocking collectives: 11.1 us -> 0 us
  other arithmetic: 8.16 us -> 5.24 us
    reduce_scatter x1 -> x0, waiting for transfers between devices: 33.6 us -> none  [body(): lax.psum_scatter(partial_value, 'tp', scatter_dimension=1, tiled=True)]
    all_to_all x1 -> x0, blocking collectives: 11.1 us -> none  [body(): gated_local = lax.all_to_all(gated_slots, 'ctx', 0, 1, tiled=True)]
    ppermute x0 -> x2, waiting for transfers between devices: none -> 10.6 us  [the longest x1 9.41 us: body(): recv_high = lax.ppermute(p_other, 'tp', [(i, i ^ 2) for i in range(n_tp)])]
    all_to_all x3 -> x2, starting transfers between devices: 21.3 us -> 13.6 us  [the longest x1 9.71 us: body(): arrived = lax.all_to_all(packed, 'ctx', 1, 0, tiled=True).T]
    ppermute x0 -> x2, starting transfers between devices: none -> 6.59 us  [the longest x1 3.89 us: body(): recv_core = lax.ppermute(send_core, 'tp', [(i, i ^ 1) for i in range(n_tp)])]
    all_to_all x3 -> x2, waiting for transfers between devices: 13.7 us -> 13.4 us  [the longest x1 7.55 us: body(): gated_local = lax.all_to_all(gated_slots, 'ctx', 0, 1, tiled=True)]
  transfers between devices with their start and end apart: 4 -> 4, of which waited for: 3 -> 4; matrix products, arithmetic and copies ran while one was open for 8% -> 5% of each run, Pallas kernels for 0% -> 0%
where the time goes in v3:
time: 76.3 us; the launch traced here: 74.9 us
  waiting for transfers between devices  23.9 us (31%)
  starting transfers between devices  20.2 us (26%)
  Pallas kernels  13.9 us (18%)
  local copies, waits for them, and re-layouts  10.7 us (14%)
  other arithmetic  5.24 us (7%)
    pallas_call x1, Pallas kernels, pallas_conv(): pl.pallas_call(conv_kernel, grid=(chans,), in_specs=[pl.BlockSpec((1, 1,...  13.9 us
    all_to_all x1, starting transfers between devices, body(): arrived = lax.all_to_all(packed, 'ctx', 1, 0, tiled=True).T  9.71 us
    ppermute x1, waiting for transfers between devices, body(): recv_high = lax.ppermute(p_other, 'tp', [(i, i ^ 2) for i in range(n_tp)])  9.41 us
    all_to_all x1, waiting for transfers between devices, body(): gated_local = lax.all_to_all(gated_slots, 'ctx', 0, 1, tiled=True)  7.55 us
    all_to_all x1, waiting for transfers between devices, body(): arrived = lax.all_to_all(packed, 'ctx', 1, 0, tiled=True).T  5.81 us
    ppermute x1, starting transfers between devices, body(): recv_core = lax.ppermute(send_core, 'tp', [(i, i ^ 1) for i in range(n_tp)])  3.89 us
    all_to_all x1, starting transfers between devices, body(): gated_local = lax.all_to_all(gated_slots, 'ctx', 0, 1, tiled=True)  3.86 us
    unnamed x11, local copies, waits for them, and re-layouts  3.23 us
  transfers between devices with their start and end apart: 4, of which 4 were waited for; matrix products, arithmetic and copies ran while one was open for 5% of the time, Pallas kernels for 0%

profile of v3, /device:TPU:1, one launch (start us, length us, event | category | flops | bytes accessed | tf_op | source)
XLA Modules:
  0.0 74.9 jit_solution(6070019422720053399)
XLA Ops:
  0.0 1.2 %copy.54 = bf16[128,512]{0,1:T(8,128)(2,1)S(1)} copy(bf16[128,512]{1,0:T(8,128)(2,1)} %param.9) | data formatting | bytes 262144 | tf_op args[0]
  1.2 1.0 %copy.55 = bf16[128,512]{0,1:T(8,128)(2,1)S(1)} copy(bf16[128,512]{1,0:T(8,128)(2,1)} %param.10) | data formatting | bytes 262144 | tf_op args[1]
  2.2 1.0 %copy.56 = bf16[128,512]{0,1:T(8,128)(2,1)S(1)} copy(bf16[128,512]{1,0:T(8,128)(2,1)} %param.11) | data formatting | bytes 262144 | tf_op args[2]
  3.3 0.8 %copy.57 = bf16[128,32,3,16]{0,3,2,1:T(8,128)(2,1)} copy(bf16[128,32,3,16]{0,3,1,2:T(8,128)(2,1)S(1)} %pad_maximum_fusion) | data formatting | bytes 786432 | tf_op jit(solution)/shard_map/stack | solution.py:82
  4.1 9.7 %all-to-all-start = ((bf16[128,32,48]{0,2,1:T(8,128)(2,1)}), bf16[128,32,48]{0,2,1:T(8,128)(2,1)S(1)}, u32[]{:S(2)}, u32[]{:S(2)}) async-start(bf16[128,32,48]{0,2,1:T(8,128)(2,1)} %bitcast.3), calls=%async_computation | async-start | bytes 786432 | tf_op jit(solution)/shard_map/all_to_all | solution.py:85
  13.9 0.8 %scatter_custom_fusion = s32[64]{0:T(128)S(1)} fusion(s32[64]{0:T(128)S(1)} %compare_select_fusion, s32[64]{0:T(128)S(1)} %iota.20, s32[]{:T(128)} %constant.46.clone.1), kind=kCustom, calls=%fused_computation.35 | custom fusion | bytes 260 | tf_op jit(solution)/shard_map/scatter | solution.py:77
  15.5 1.7 %and_convert_fusion.mz_ref = f32[2,64,4096]{2,1,0:T(8,128)} fusion(s32[2,64]{1,0:T(2,128)S(1)} %convert_reduce_fusion, s32[64,4096]{1,0:T(8,128)S(1)} %iota_add_fusion, pred[4096]{0:T(1024)(128)(4,1)S(1)} %iota_compare_fusion), kind=kLoop, calls=%fused_computation.5 | loop fusion | flops 1572864 | bytes 3150336 | tf_op jit(solution)/shard_map/convert_element_type | solution.py:52
  17.2 0.8 %dynamic_slice.15 = f32[16]{0:T(128)S(1)} dynamic-slice(f32[512]{0:T(512)} %param.12, s32[]{:T(128)S(6)} %select_n.37), dynamic_slice_sizes={16} | dynamic-slice | bytes 132 | tf_op jit(solution)/shard_map/dynamic_slice | solution.py:89
  18.0 5.8 %all-to-all-done = bf16[128,32,48]{0,2,1:T(8,128)(2,1)S(1)} async-done(((bf16[128,32,48]{0,2,1:T(8,128)(2,1)}), bf16[128,32,48]{0,2,1:T(8,128)(2,1)S(1)}, u32[]{:S(2)}, u32[]{:S(2)}) %all-to-all-start) | async-done | bytes 393248 | tf_op jit(solution)/shard_map/all_to_all | solution.py:85
  24.3 0.9 %copy.63.f_ref = bf16[16,1,4224]{2,1,0:T(2,128)(2,1)} copy(bf16[16,1,4224]{2,0,1:T(8,128)(2,1)S(1)} %pad_bitcast_fusion) | data formatting | bytes 270336 | tf_op jit(solution)/shard_map/reshape | solution.py:46
  25.6 0.6 gather_fusion.1
  26.3 0.6 gather_fusion
  26.9 0.8 %fusion.3.x_ref = bf16[16,64,64]{2,1,0:T(8,128)(2,1)} fusion(bf16[64,16,64]{2,1,0:T(8,128)(2,1)S(1)} %gather_fusion.1, pred[64]{0:T(512)(128)(4,1)S(1)} %get-tuple-element.12), kind=kLoop, calls=%fused_computation.15 | loop fusion | flops 65536 | bytes 262208 | tf_op jit(solution)/shard_map/jit(_take)/select_n | solution.py:80
  27.7 13.9 %shard_map.73 = f32[16,64,64]{2,1,0:T(8,128)} custom-call(bf16[16,1,4224]{2,1,0:T(2,128)(2,1)} %copy.63.f_ref, bf16[16,64,64]{2,1,0:T(8,128)(2,1)} %fusion.3.x_ref, s32[64,64]{1,0:T(8,128)} %copy-done.1, f32[2,64,4096]{2,1,0:T(8,128)} %and_convert_fusion.mz_ref), custom_call_target="tpu_custom_call" | custom-call | tf_op jit(solution)/shard_map/pallas_call | solution.py:53
  41.6 1.3 %multiply_convert_fusion = bf16[16,64,64]{2,1,0:T(8,128)(2,1)S(1)} fusion(f32[16,64,64]{2,1,0:T(8,128)} %shard_map.73, bf16[64,16,64]{2,1,0:T(8,128)(2,1)S(1)} %gather_fusion, f32[16]{0:T(128)S(1)} %dynamic_slice.15, pred[64]{0:T(512)(128)(4,1)S(1)} %get-tuple-element.12, bf16[64,16,64]{2,1,0:T(8,128)(2,1)S(1)} %gather_fusion.1), kind=kLoop, calls=%fused_computation.11 | loop fusion | flops 524288 | bytes 655488 | tf_op jit(solution)/shard_map/convert_element_type | solution.py:93
  43.0 0.6 gather_fusion.2
  44.2 0.7 copy_bitcast_fusion
  44.9 3.9 %all-to-all-start.1 = ((bf16[32,128,16]{1,2,0:T(8,128)(2,1)}), bf16[32,128,16]{1,2,0:T(8,128)(2,1)S(1)}, u32[]{:S(2)}, u32[]{:S(2)}) async-start(bf16[32,128,16]{1,2,0:T(8,128)(2,1)} %copy_bitcast_fusion), calls=%async_computation.1 | async-start | bytes 262144 | tf_op jit(solution)/shard_map/all_to_all | solution.py:96
  48.7 7.5 %all-to-all-done.1 = bf16[32,128,16]{1,2,0:T(8,128)(2,1)S(1)} async-done(((bf16[32,128,16]{1,2,0:T(8,128)(2,1)}), bf16[32,128,16]{1,2,0:T(8,128)(2,1)S(1)}, u32[]{:S(2)}, u32[]{:S(2)}) %all-to-all-start.1) | async-done | bytes 131104 | tf_op jit(solution)/shard_map/all_to_all | solution.py:96
  56.6 2.7 %collective-permute-start = (f32[128,1024]{1,0:T(8,128)S(1)}, f32[128,1024]{1,0:T(8,128)S(1)}, u32[]{:S(2)}, u32[]{:S(2)}) collective-permute-start(f32[128,1024]{1,0:T(8,128)S(1)} %fusion), channel_id=1, source_target_pairs={{0,2},{1,3},{2,0},{3,1},{4,6},{5,7},{6,4},{7,5},{8,10},{9,11},{10,... | collective-permute-start | bytes 1572872 | tf_op jit(solution)/shard_map/ppermute | solution.py:103
  59.3 9.4 %collective-permute-done = f32[128,1024]{1,0:T(8,128)S(1)} collective-permute-done((f32[128,1024]{1,0:T(8,128)S(1)}, f32[128,1024]{1,0:T(8,128)S(1)}, u32[]{:S(2)}, u32[]{:S(2)}) %collective-permute-start) | collective-permute-done | bytes 524320 | tf_op jit(solution)/shard_map/ppermute | solution.py:103
  69.1 3.9 %collective-permute-start.1 = (f32[128,512]{1,0:T(8,128)S(1)}, f32[128,512]{1,0:T(8,128)S(1)}, u32[]{:S(2)}, u32[]{:S(2)}) collective-permute-start(f32[128,512]{1,0:T(8,128)S(1)} %constant_dynamic-slice_fusion), channel_id=1, source_target_pairs={{0,1},{1,0},{2,3},{3,2},{4,5},{5,4},{6,7},{7,6},{8,9},{9,8},{10,11... | collective-permute-start | bytes 786440 | tf_op jit(solution)/shard_map/ppermute | solution.py:108
  73.0 1.2 %collective-permute-done.1 = f32[128,512]{1,0:T(8,128)S(1)} collective-permute-done((f32[128,512]{1,0:T(8,128)S(1)}, f32[128,512]{1,0:T(8,128)S(1)}, u32[]{:S(2)}, u32[]{:S(2)}) %collective-permute-start.1) | collective-permute-done | bytes 262176 | tf_op jit(solution)/shard_map/ppermute | solution.py:108
  74.2 0.7 add_convert_fusion
  (36 shorter events, 3.1 us)
Async XLA Ops:
  0.0 56.3 %copy-start = (bf16[512,2048]{1,0:T(8,128)(2,1)S(1)}, bf16[512,2048]{1,0:T(8,128)(2,1)}, u32[]{:S(2)}) copy-start(bf16[512,2048]{1,0:T(8,128)(2,1)} %param.15) | copy-start | bytes 6291460
  0.0 13.8 %copy-start.3 = (s32[64]{0:T(128)S(1)}, s32[64]{0:T(128)}, u32[]{:S(2)}) copy-start(s32[64]{0:T(128)} %param.14) | copy-start | bytes 772
  0.0 14.6 %copy-start.2 = (s32[4096]{0:T(1024)S(1)}, s32[4096]{0:T(1024)}, u32[]{:S(2)}) copy-start(s32[4096]{0:T(1024)} %param.13) | copy-start | bytes 49156
  4.1 19.7 %all-to-all-start = ((bf16[128,32,48]{0,2,1:T(8,128)(2,1)}), bf16[128,32,48]{0,2,1:T(8,128)(2,1)S(1)}, u32[]{:S(2)}, u32[]{:S(2)}) async-start(bf16[128,32,48]{0,2,1:T(8,128)(2,1)} %bitcast.3), calls=%async_computation | async-start | bytes 786432 | tf_op jit(solution)/shard_map/all_to_all | solution.py:85
  14.7 2.4 %copy-start.1 = (s32[64,64]{1,0:T(8,128)}, s32[64,64]{1,0:T(8,128)S(1)}, u32[]{:S(2)}) copy-start(s32[64,64]{1,0:T(8,128)S(1)} %reshape.60.doc_ref) | copy-start | bytes 49156
  44.9 11.4 %all-to-all-start.1 = ((bf16[32,128,16]{1,2,0:T(8,128)(2,1)}), bf16[32,128,16]{1,2,0:T(8,128)(2,1)S(1)}, u32[]{:S(2)}, u32[]{:S(2)}) async-start(bf16[32,128,16]{1,2,0:T(8,128)(2,1)} %copy_bitcast_fusion), calls=%async_computation.1 | async-start | bytes 262144 | tf_op jit(solution)/shard_map/all_to_all | solution.py:96
  56.6 12.1 %collective-permute-start = (f32[128,1024]{1,0:T(8,128)S(1)}, f32[128,1024]{1,0:T(8,128)S(1)}, u32[]{:S(2)}, u32[]{:S(2)}) collective-permute-start(f32[128,1024]{1,0:T(8,128)S(1)} %fusion), channel_id=1, source_target_pairs={{0,2},{1,3},{2,0},{3,1},{4,6},{5,7},{6,4},{7,5},{8,10},{9,11},{10,... | collective-permute-start | bytes 1572872 | tf_op jit(solution)/shard_map/ppermute | solution.py:103
  69.1 5.1 %collective-permute-start.1 = (f32[128,512]{1,0:T(8,128)S(1)}, f32[128,512]{1,0:T(8,128)S(1)}, u32[]{:S(2)}, u32[]{:S(2)}) collective-permute-start(f32[128,512]{1,0:T(8,128)S(1)} %constant_dynamic-slice_fusion), channel_id=1, source_target_pairs={{0,1},{1,0},{2,3},{3,2},{4,5},{5,4},{6,7},{7,6},{8,9},{9,8},{10,11... | collective-permute-start | bytes 786440 | tf_op jit(solution)/shard_map/ppermute | solution.py:108
